TPU v7x, 32 devices: a whole 2x2x4 slice. The times are simulated.
32 devices in a mesh: tm: 4 (over y, core), chan: 8 (over z, x).
Axes of the slice: x: 2, y: 2, z: 4, core: 2. Of those that a mesh axis runs over, the one named last changes fastest.
Arguments:
- traces: bfloat16 [8, 1024, 1024], P('tm', 'chan'), may hold values from -6 to 6
- lengths: int32 [8], replicated, may hold values from 512 to 1024
- source_blocks: int32 [3], replicated, may hold values from 0 to 31
Outputs:
- stacks: float32 [32, 3, 201, 1024], P('tm', None, None, 'chan')
Inputs may be any that keep to these rules, and one draw needn't show every extreme that they name: Step s takes the source channels 32 * source_blocks[s] to 32 * source_blocks[s] + 31. `lengths`: samples at and after a segment's length are not used.
All inputs are finite; a program needn't handle non-finite values.
Results may differ from a plain program's by a relative error of at most 0.0085.
Values may be sent and summed in bfloat16 or wider, within the bound.
No kernel may reach another device: no remote copies, remote signals or barrier semaphores. Data moves between devices by JAX's collectives and lax.ppermute only.
A program may use at most 256 MiB of HBM per device.

v0:
```python
import jax
import jax.numpy as jnp
from jax import lax
from jax.sharding import PartitionSpec as P

MAXLAG = 100
SRC = 32


epsilon = 1e-06


def whiten(traces, lengths):
    sample_len = traces.shape[2]
    positions = lax.broadcasted_iota(jnp.int32, (1, 1, sample_len), 2)
    valid_mask = (positions < lengths[:, None, None]).astype(jnp.float32)
    masked = traces.astype(jnp.float32) * valid_mask
    seg_count = lengths.astype(jnp.float32)[:, None, None]
    mean_power = jnp.sum(masked * masked, axis=2, keepdims=True) / seg_count
    return (masked / jnp.sqrt(mean_power + epsilon)).astype(jnp.bfloat16)


def correlate(sources, receivers, lengths):
    sample_len = sources.shape[2]
    padded = jnp.pad(sources, ((0, 0), (0, 0), (MAXLAG, MAXLAG)))
    root_count = jnp.sqrt(lengths.astype(jnp.float32))
    lag_total = 2 * MAXLAG + 1
    lag_blocks = []
    for start_lag in range(0, lag_total, 67):
        lag_width = min(67, lag_total - start_lag)
        offsets = start_lag + jnp.arange(lag_width, dtype=jnp.int32)

        def take_lag(lag_value):
            return lax.dynamic_slice_in_dim(padded, 2 * MAXLAG - lag_value, sample_len, 2)

        shifted = jax.vmap(take_lag, out_axes=2)(offsets)
        product = jnp.einsum(
            "gnau,gcu->gnac", shifted, receivers, preferred_element_type=jnp.float32
        )
        lag_blocks.append(jnp.sum(product / root_count[:, None, None, None], axis=0))
    return jnp.concatenate(lag_blocks, axis=1)


def shards(traces, lengths, source_blocks):
    seg_dev = traces.shape[0]
    own_lengths = lax.dynamic_slice_in_dim(lengths, lax.axis_index("tm") * seg_dev, seg_dev, 0)
    whitened = whiten(traces, own_lengths)
    per_owner = whitened.shape[1] // SRC
    step_count = source_blocks.shape[0]
    sources = []
    my_index = lax.axis_index("chan")
    contributions = []
    for step_index in range(step_count):
        owner_index = source_blocks[step_index] // per_owner
        local_start = source_blocks[step_index] % per_owner * SRC
        block_here = lax.dynamic_slice_in_dim(whitened, local_start, SRC, 1).astype(jnp.float32)
        contributions.append(
            jnp.where(owner_index == my_index, block_here, jnp.zeros_like(block_here))
        )
    summed = lax.psum(jnp.stack(contributions), "chan")
    sources = [summed[step_index].astype(jnp.bfloat16) for step_index in range(step_count)]
    results = []
    for step_index in range(step_count):
        chosen = sources[step_index]
        results.append(
            lax.psum_scatter(
                correlate(chosen, whitened, own_lengths).astype(jnp.bfloat16),
                "tm",
                scatter_dimension=0,
                tiled=True,
            ).astype(jnp.float32)
        )
    return jnp.stack(results, axis=1)


def solution(mesh):
    return jax.shard_map(
        shards,
        mesh=mesh,
        in_specs=(P("tm", "chan", None), P(), P()),
        out_specs=P("tm", None, None, "chan"),
        check_vma=False,
    )
```

profile of v0, /device:TPU:0, one launch (start us, length us, event | category | flops | bytes accessed | tf_op | source)
XLA Modules:
  0.0 1519.1 jit_solution(4298698127265527890)
XLA Ops:
  19.2 47.3 %all-reduce.14 = bf16[3,2,32,1024]{3,2,1,0:T(8,128)(2,1)S(1)} all-reduce(f32[3,2,32,1024]{3,2,1,0:T(8,128)S(1)} %pad_maximum_fusion.3), channel_id=1, replica_groups=mesh['tm'=4,'chan'=8] {'chan'}, use_global_device_ids=true, to_apply=%region_1.2 | all-reduce | flops 196608 | bytes 1179648 | tf_op jit(solution)/shard_map/psum | solution.py:60
  66.7 4.5 broadcast.153.clone
  71.2 128.9 %while.9 = (s32[]{:T(128)}, bf16[2,32,1224]{2,1,0:T(8,128)(2,1)S(1)}, s32[67,3]{0,1:T(4,128)S(1)}, bf16[67,2,32,1024]{3,2,1,0:T(8,128)(2,1)}, s32[]{:T(128)}) while((s32[]{:T(128)}, bf16[2,32,1224]{2,1,0:T(8,128)(2,1)S(1)}, s32[67,3]{0,1:T(4,128)S(1)}, bf16[67,2,32,1024]{3,2,1,0:T(8,128)(2,1)}, s32[]{:T(128)}) %tuple.120), condition=%wide.while_cond, body=%wide.while_body.sunk | while | flops 2 | bytes 262765 | solution.py:34
  200.1 5.9 fusion.16
  206.1 4.5 broadcast.153.clone.1
  210.5 133.6 %while.10 = (s32[]{:T(128)}, bf16[2,32,1224]{2,1,0:T(8,128)(2,1)S(1)}, s32[67,3]{0,1:T(4,128)S(1)}, bf16[67,2,32,1024]{3,2,1,0:T(8,128)(2,1)}, s32[]{:T(128)}) while((s32[]{:T(128)}, bf16[2,32,1224]{2,1,0:T(8,128)(2,1)S(1)}, s32[67,3]{0,1:T(4,128)S(1)}, bf16[67,2,32,1024]{3,2,1,0:T(8,128)(2,1)}, s32[]{:T(128)}) %tuple.150), condition=%wide.while_cond.1, body=%wide.while_body.1.sunk | while | flops 2 | bytes 262765 | solution.py:34
  344.1 7.3 fusion.14
  351.4 4.5 broadcast.153.clone.2
  355.9 134.0 %while.11 = (s32[]{:T(128)}, bf16[2,32,1224]{2,1,0:T(8,128)(2,1)S(1)}, s32[67,3]{0,1:T(4,128)S(1)}, bf16[67,2,32,1024]{3,2,1,0:T(8,128)(2,1)}, s32[]{:T(128)}) while((s32[]{:T(128)}, bf16[2,32,1224]{2,1,0:T(8,128)(2,1)S(1)}, s32[67,3]{0,1:T(4,128)S(1)}, bf16[67,2,32,1024]{3,2,1,0:T(8,128)(2,1)}, s32[]{:T(128)}) %tuple.151), condition=%wide.while_cond.2, body=%wide.while_body.2.sunk | while | flops 2 | bytes 262765 | solution.py:34
  489.9 7.4 fusion.12
  497.4 4.5 broadcast.153.clone.3
  501.9 127.6 %while.12 = (s32[]{:T(128)}, bf16[2,32,1224]{2,1,0:T(8,128)(2,1)S(1)}, s32[67,3]{0,1:T(4,128)S(1)}, bf16[67,2,32,1024]{3,2,1,0:T(8,128)(2,1)}, s32[]{:T(128)}) while((s32[]{:T(128)}, bf16[2,32,1224]{2,1,0:T(8,128)(2,1)S(1)}, s32[67,3]{0,1:T(4,128)S(1)}, bf16[67,2,32,1024]{3,2,1,0:T(8,128)(2,1)}, s32[]{:T(128)}) %tuple.156), condition=%wide.while_cond.3, body=%wide.while_body.3.sunk | while | flops 2 | bytes 262765 | solution.py:34
  629.5 7.3 fusion.10
  636.8 4.5 broadcast.153.clone.4
  641.3 141.5 %while.13 = (s32[]{:T(128)}, bf16[2,32,1224]{2,1,0:T(8,128)(2,1)S(1)}, s32[67,3]{0,1:T(4,128)S(1)}, bf16[67,2,32,1024]{3,2,1,0:T(8,128)(2,1)}, s32[]{:T(128)}) while((s32[]{:T(128)}, bf16[2,32,1224]{2,1,0:T(8,128)(2,1)S(1)}, s32[67,3]{0,1:T(4,128)S(1)}, bf16[67,2,32,1024]{3,2,1,0:T(8,128)(2,1)}, s32[]{:T(128)}) %tuple.158), condition=%wide.while_cond.4, body=%wide.while_body.4.sunk | while | flops 2 | bytes 262765 | solution.py:34
  646.2 1.5 bitcast_dynamic-update-slice_fusion.22
  656.8 1.5 bitcast_dynamic-update-slice_fusion.22
  673.7 1.5 bitcast_dynamic-update-slice_fusion.22
  686.3 1.5 bitcast_dynamic-update-slice_fusion.22
  696.9 1.5 bitcast_dynamic-update-slice_fusion.22
  707.4 1.5 bitcast_dynamic-update-slice_fusion.22
  715.9 1.5 bitcast_dynamic-update-slice_fusion.22
  730.7 1.5 bitcast_dynamic-update-slice_fusion.22
  758.1 1.5 bitcast_dynamic-update-slice_fusion.22
  775.0 1.5 bitcast_dynamic-update-slice_fusion.22
  782.8 7.3 fusion.8
  790.1 4.5 broadcast.153.clone.5
  794.6 134.6 %while.14 = (s32[]{:T(128)}, bf16[2,32,1224]{2,1,0:T(8,128)(2,1)S(1)}, s32[67,3]{0,1:T(4,128)S(1)}, bf16[67,2,32,1024]{3,2,1,0:T(8,128)(2,1)}, s32[]{:T(128)}) while((s32[]{:T(128)}, bf16[2,32,1224]{2,1,0:T(8,128)(2,1)S(1)}, s32[67,3]{0,1:T(4,128)S(1)}, bf16[67,2,32,1024]{3,2,1,0:T(8,128)(2,1)}, s32[]{:T(128)}) %tuple.160), condition=%wide.while_cond.5, body=%wide.while_body.5.sunk | while | flops 2 | bytes 262765 | solution.py:34
  929.2 7.3 fusion.6
  936.6 4.5 broadcast.153.clone.6
  941.1 132.3 %while.15 = (s32[]{:T(128)}, bf16[2,32,1224]{2,1,0:T(8,128)(2,1)S(1)}, s32[67,3]{0,1:T(4,128)S(1)}, bf16[67,2,32,1024]{3,2,1,0:T(8,128)(2,1)}, s32[]{:T(128)}) while((s32[]{:T(128)}, bf16[2,32,1224]{2,1,0:T(8,128)(2,1)S(1)}, s32[67,3]{0,1:T(4,128)S(1)}, bf16[67,2,32,1024]{3,2,1,0:T(8,128)(2,1)}, s32[]{:T(128)}) %tuple.157), condition=%wide.while_cond.6, body=%wide.while_body.6.sunk | while | flops 2 | bytes 262765 | solution.py:34
  1073.4 7.3 fusion.4
  1080.7 4.5 broadcast.153.clone.7
  1085.2 141.9 %while.16 = (s32[]{:T(128)}, bf16[2,32,1224]{2,1,0:T(8,128)(2,1)S(1)}, s32[67,3]{0,1:T(4,128)S(1)}, bf16[67,2,32,1024]{3,2,1,0:T(8,128)(2,1)}, s32[]{:T(128)}) while((s32[]{:T(128)}, bf16[2,32,1224]{2,1,0:T(8,128)(2,1)S(1)}, s32[67,3]{0,1:T(4,128)S(1)}, bf16[67,2,32,1024]{3,2,1,0:T(8,128)(2,1)}, s32[]{:T(128)}) %tuple.159), condition=%wide.while_cond.7, body=%wide.while_body.7.sunk | while | flops 2 | bytes 262765 | solution.py:34
  1088.0 1.5 bitcast_dynamic-update-slice_fusion.25
  1090.1 1.5 bitcast_dynamic-update-slice_fusion.25
  1100.7 1.5 bitcast_dynamic-update-slice_fusion.25
  1104.9 1.5 bitcast_dynamic-update-slice_fusion.25
  1109.2 1.5 bitcast_dynamic-update-slice_fusion.25
  1117.6 1.5 bitcast_dynamic-update-slice_fusion.25
  1119.8 1.5 bitcast_dynamic-update-slice_fusion.25
  1130.3 1.5 bitcast_dynamic-update-slice_fusion.25
  1140.9 1.5 bitcast_dynamic-update-slice_fusion.25
  1151.5 1.5 bitcast_dynamic-update-slice_fusion.25
  1160.0 1.5 bitcast_dynamic-update-slice_fusion.25
  1162.1 1.5 bitcast_dynamic-update-slice_fusion.25
  1168.4 1.5 bitcast_dynamic-update-slice_fusion.25
  1174.8 1.5 bitcast_dynamic-update-slice_fusion.25
  1179.1 1.5 bitcast_dynamic-update-slice_fusion.25
  1181.2 1.5 bitcast_dynamic-update-slice_fusion.25
  1183.3 1.5 bitcast_dynamic-update-slice_fusion.25
  1202.4 1.5 bitcast_dynamic-update-slice_fusion.25
  1219.3 1.5 bitcast_dynamic-update-slice_fusion.25
  1221.4 1.5 bitcast_dynamic-update-slice_fusion.25
  1227.1 7.3 fusion.2
  1234.4 4.5 broadcast.153.clone.8
  1238.9 134.3 %while.17 = (s32[]{:T(128)}, bf16[2,32,1224]{2,1,0:T(8,128)(2,1)S(1)}, s32[67,3]{0,1:T(4,128)S(1)}, bf16[67,2,32,1024]{3,2,1,0:T(8,128)(2,1)}, s32[]{:T(128)}) while((s32[]{:T(128)}, bf16[2,32,1224]{2,1,0:T(8,128)(2,1)S(1)}, s32[67,3]{0,1:T(4,128)S(1)}, bf16[67,2,32,1024]{3,2,1,0:T(8,128)(2,1)}, s32[]{:T(128)}) %tuple.161), condition=%wide.while_cond.8, body=%wide.while_body.8.sunk | while | flops 2 | bytes 262765 | solution.py:34
  1373.2 7.5 fusion
  1380.7 22.0 %fusion.26 = (bf16[32,67,128]{2,1,0:T(8,128)(2,1)S(1)}, bf16[32,67,128]{2,1,0:T(8,128)(2,1)S(1)}, bf16[32,67,128]{2,1,0:T(8,128)(2,1)S(1)}, bf16[32,67,128]{2,1,...) fusion(f32[2,32,67,128]{3,1,2,0:T(8,128)S(1)} %fusion.16, ...), kind=kLoop, calls=%fused_computation.53 | loop fusion | flops 7409664 | bytes 24698888 | tf_op jit(solution)/shard_map/reduce_sum | solution.py:40
  1403.2 1.6 copy.24
  1405.2 1.7 copy.20
  1407.3 1.6 copy.16
  1410.3 96.7 %all-reduce.13.cloned.1.call-done = (bf16[32,201,128]{2,0,1:T(8,128)(2,1)}, bf16[32,201,128]{2,0,1:T(8,128)(2,1)}, bf16[32,201,128]{2,0,1:T(8,128)(2,1)}) async-done(((bf16[32,201,128]{2,0,1:T(8,128)(2,1)}, bf16[32,201,128]{2,0,1:T(8,128)(2,1)}, bf16[32,201,128]{2,0,1:T(8,128)(2,1)}), (bf16[32,201,128]{2,0,1:T(8,128)(2,1)}, bf16[32,201,128]{2,0,1:T(8,128)(2,1)}, ...) | async-done | bytes 4939792
  1510.1 1.6 maximum_convert_fusion
  (1812 shorter events, 1174.1 us)
Async XLA Ops:
  6.5 1500.5 %all-reduce.13.cloned.1.call-start = ((), (), s32[]{:S(2)}) async-start(), calls=%async_computation | async-start | bytes 9879552
  1373.2 7.5 copy-start
  1373.2 7.5 copy-start.1
  1404.8 4.2 copy-start.2
Sparse Core Ops, SparseCore 0:
  1409.1 97.8 all-reduce.12
where the time goes:
time: 1530 us; the launch traced here: 1520 us
  local copies, waits for them, and re-layouts  1260 us (82%)
  waiting for transfers between devices  96.7 us (6%)
  matrix products  64.7 us (4%)
  blocking collectives  47.3 us (3%)
  other arithmetic  28.5 us (2%)
  between operations  22.4 us (1%)
    gather x1809, local copies, waits for them, and re-layouts  1210 us
    unnamed x2, waiting for transfers between devices  96.7 us
    dot_general x9, matrix products, correlate(): jnp.einsum('gnau,gcu->gnac', shifted, receivers, preferred_element_type=j...  64.7 us
    psum x1, blocking collectives, shards(): summed = lax.psum(jnp.stack(contributions), 'chan')  47.3 us
    unnamed x16, local copies, waits for them, and re-layouts  41.1 us
  transfers between devices with their start and end apart: 1, of which 1 were waited for; matrix products, arithmetic and copies ran while one was open for 0% of the time, Pallas kernels for 0%

commit v1 on v0

v1 whole, which is shorter than its diff:
```python
import functools

import jax
import jax.numpy as jnp
from jax import lax
from jax.experimental import pallas as pl
from jax.experimental.pallas import tpu as pltpu
from jax.sharding import Mesh
from jax.sharding import PartitionSpec as P

MAXLAG = 100
SRC = 32
FINE = 16
LANES = 128
GROUP = 2
NEAR = 4
epsilon = 1e-06

SMEM = pl.BlockSpec(memory_space=pltpu.SMEM)
VMEM = pl.BlockSpec(memory_space=pltpu.VMEM)
HBM = pl.BlockSpec(memory_space=pltpu.HBM)
SMALL = pltpu.CompilerParams(vmem_limit_bytes=8 << 20)
WHOLE = pltpu.CompilerParams(vmem_limit_bytes=60 << 20)
LARGE = pltpu.CompilerParams(vmem_limit_bytes=28 << 20)


def plan(samp):
    lags = 2 * MAXLAG + 1
    blocks = -(-lags // FINE)
    front = -(-MAXLAG // FINE) * FINE
    base = front - MAXLAG
    tail = -(-(base + FINE - 1) // FINE) * FINE
    rows = samp + (blocks - 1) * FINE + tail
    return lags, blocks, front, base, tail, rows


def extract_kernel(per_owner, blocks_hbm, traces_ref, out_ref, owner_ref, blocks_ref, buf, sems):
    steps = blocks_ref.shape[0]
    seg_dev, _, samp = traces_ref.shape
    _, rows, width = out_ref.shape
    share = rows // steps
    load = pltpu.make_async_copy(blocks_hbm, blocks_ref, sems.at[steps * seg_dev])
    load.start()
    load.wait()
    copies = []
    for s in range(steps):
        first = pl.multiple_of(lax.rem(blocks_ref[s], per_owner) * SRC, SRC)
        for g in range(seg_dev):
            n = s * seg_dev + g
            copy = pltpu.make_async_copy(
                traces_ref.at[g, pl.ds(first, SRC), :], buf.at[n], sems.at[n]
            )
            copy.start()
            copies.append(copy)
        owner_ref[s] = jnp.full(owner_ref.shape[1:], lax.div(blocks_ref[s], per_owner), jnp.int32)
    for s in range(steps):
        for g in range(seg_dev):
            n = s * seg_dev + g
            copies[n].wait()
            for q in range(SRC // share):
                for h in range(samp // width):
                    out_ref[(q * (samp // width) + h) * seg_dev + g, s * share:(s + 1) * share, :] = buf[
                        n, q * share:(q + 1) * share, h * width:(h + 1) * width
                    ]


def extract(traces, source_blocks, n_tm):
    seg_dev, chans, samp = traces.shape
    steps = source_blocks.shape[0]
    share = SRC // n_tm
    return pl.pallas_call(
        functools.partial(extract_kernel, chans // SRC),
        out_shape=(
            jax.ShapeDtypeStruct((n_tm * 2 * seg_dev, steps * share, samp // 2), traces.dtype),
            jax.ShapeDtypeStruct((steps, share, LANES), jnp.int32),
        ),
        in_specs=[HBM, HBM],
        out_specs=(VMEM, VMEM),
        scratch_shapes=[
            pltpu.SMEM((steps,), jnp.int32),
            pltpu.VMEM((steps * seg_dev, SRC, samp), traces.dtype),
            pltpu.SemaphoreType.DMA((steps * seg_dev + 1,)),
        ],
        compiler_params=WHOLE,
        name="extract",
    )(source_blocks, traces)


def pick_kernel(owner_ref, got_ref, out_ref):
    steps, share, _ = owner_ref.shape
    n_tm, _, width = out_ref.shape
    near = got_ref.shape[0] // n_tm
    for s in range(steps):
        rows = slice(s * share, (s + 1) * share)
        owner = owner_ref[s] & (near - 1)
        for q in range(n_tm):
            for c in range(0, width, LANES):
                taken = got_ref[q * near, rows, c:c + LANES].astype(jnp.float32)
                for b in range(1, near):
                    other = got_ref[q * near + b, rows, c:c + LANES].astype(jnp.float32)
                    taken = jnp.where(owner == b, other, taken)
                out_ref[q, rows, c:c + LANES] = taken.astype(out_ref.dtype)


def pick(got, owners, n_tm):
    return pl.pallas_call(
        pick_kernel,
        out_shape=jax.ShapeDtypeStruct((n_tm,) + got.shape[1:], got.dtype),
        in_specs=[VMEM, VMEM],
        out_specs=VMEM,
        compiler_params=SMALL,
        name="pick",
    )(owners, got)


def choose_kernel(bit, owner_ref, held_ref, came_ref, out_ref):
    steps, share, _ = owner_ref.shape
    n_tm, _, width = out_ref.shape
    here = lax.axis_index("zh") * NEAR
    for s in range(steps):
        rows = slice(s * share, (s + 1) * share)
        other = ((owner_ref[s] ^ here) & (bit * NEAR)) != 0
        for q in range(n_tm):
            for c in range(0, width, LANES):
                held = held_ref[q, rows, c:c + LANES].astype(jnp.float32)
                came = came_ref[q, rows, c:c + LANES].astype(jnp.float32)
                out_ref[q, rows, c:c + LANES] = jnp.where(other, came, held).astype(out_ref.dtype)


def choose(held, came, owners, bit):
    return pl.pallas_call(
        functools.partial(choose_kernel, bit),
        out_shape=jax.ShapeDtypeStruct(held.shape, held.dtype),
        in_specs=[VMEM, VMEM, VMEM],
        out_specs=VMEM,
        compiler_params=SMALL,
        name="choose",
    )(owners, held, came)


def prepare_kernel(distance, len_ref, part_ref, out_ref):
    seg_dev, chans, samp = part_ref.shape
    _, _, front, _, _, rows = plan(samp)
    for g in range(seg_dev):
        count = len_ref[(lax.axis_index("tm") ^ distance) * seg_dev + g]
        xt = part_ref[g].T.astype(jnp.float32)
        pos = lax.broadcasted_iota(jnp.int32, xt.shape, 0)
        xt = jnp.where(pos < count, xt, 0.0)
        power = jnp.sum(xt * xt, axis=0, keepdims=True) / count.astype(jnp.float32)
        scale = 1.0 / jnp.sqrt(power + epsilon)
        out_ref[g, 0:front, :] = jnp.zeros((front, chans), out_ref.dtype)
        out_ref[g, front:front + samp, :] = (xt * scale).astype(out_ref.dtype)
        out_ref[g, front + samp:rows, :] = jnp.zeros((rows - front - samp, chans), out_ref.dtype)


def prepare(part, lengths, distance):
    seg_dev, chans, samp = part.shape
    rows = plan(samp)[-1]
    return pl.pallas_call(
        functools.partial(prepare_kernel, distance),
        out_shape=jax.ShapeDtypeStruct((seg_dev, rows, chans), jnp.bfloat16),
        in_specs=[SMEM, VMEM],
        out_specs=VMEM,
        compiler_params=SMALL,
        cost_estimate=pl.CostEstimate(flops=0, bytes_accessed=4 << 20, transcendentals=0),
        name="prepare",
    )(lengths, part)


def correlate_kernel(n_parts, flip, first, steps, len_ref, near_ref, far_ref, *refs):
    parts = refs[:n_parts]
    if first:
        out_ref, lhs, tailbuf = refs[n_parts:]
        carry_ref = None
    else:
        carry_ref, out_ref, buf, lhs, tailbuf, sems = refs[n_parts:]
    seg_dev, rows, chans = parts[0].shape
    _, nsrc, half = near_ref.shape
    samp = 2 * half
    share = nsrc // steps
    lags, blocks, front, base, tail, rows = plan(samp)
    bf = jnp.bfloat16
    tm_here = lax.axis_index("tm")
    local = lax.axis_index("x") ^ flip
    low_here = lax.axis_index("zl") == 0
    for m in range(n_parts):
        q = tm_here ^ m
        count = len_ref[q * seg_dev + local]
        countf = count.astype(jnp.float32)
        near = near_ref[q].astype(jnp.float32)
        far = far_ref[q].astype(jnp.float32)
        x = jnp.concatenate(
            [jnp.where(low_here, near, far), jnp.where(low_here, far, near)], axis=1
        )
        pos = lax.broadcasted_iota(jnp.int32, x.shape, 1)
        x = jnp.where(pos < count, x, 0.0)
        power = jnp.sum(x * x, axis=1, keepdims=True) / countf
        x = x / (jnp.sqrt(power + epsilon) * jnp.sqrt(countf))
        x = jnp.concatenate([x, jnp.zeros((nsrc, LANES), jnp.float32)], axis=1)
        for s in range(steps):
            rowsx = x[s * share:(s + 1) * share]
            for r in range(0, FINE, 2):
                t = jnp.concatenate(
                    [pltpu.roll(rowsx, base + r + d, 1) for d in range(2)], axis=0
                )
                at = (s * FINE + r) * share
                lhs[at:at + 2 * share, m * samp:(m + 1) * samp] = t[:, :samp].astype(bf)
                last = t[:, samp:]
                if m:
                    last = tailbuf[at:at + 2 * share, :] + pltpu.roll(last, m * tail, 1)
                if m == n_parts - 1:
                    lhs[at:at + 2 * share, n_parts * samp:] = last.astype(bf)
                else:
                    tailbuf[at:at + 2 * share, :] = last
    copies = []
    for n, k0 in enumerate(range(0, blocks, GROUP)):
        ks = range(k0, min(k0 + GROUP, blocks))

        def window(m, start, n):
            return jnp.concatenate(
                [parts[m][local, start + k * FINE:start + k * FINE + n, :] for k in ks], axis=1
            )

        acc = jnp.dot(lhs[:, 0:samp], window(0, 0, samp), preferred_element_type=jnp.float32)
        for m in range(1, n_parts):
            acc = acc + jnp.dot(
                lhs[:, m * samp:(m + 1) * samp],
                window(m, 0, samp),
                preferred_element_type=jnp.float32,
            )
        if k0 * FINE < front:
            ends = jnp.concatenate([window(m, samp, tail) for m in range(n_parts)], axis=0)
            acc = acc + jnp.dot(
                lhs[:, n_parts * samp:n_parts * (samp + tail)], ends, preferred_element_type=jnp.float32
            )
        width = len(ks) * chans
        if first:
            out_ref[n, :, 0:width] = acc
            continue
        acc = acc + carry_ref[n, :, 0:width]
        for p, k in enumerate(ks):
            high = min(FINE, lags - k * FINE)
            for s in range(steps):
                block = acc[s * FINE * share:(s * FINE + high) * share, p * chans:(p + 1) * chans]
                buf[s, k * FINE:k * FINE + high, :, :] = block.reshape(high, share, chans)
        lag0, lag1 = k0 * FINE, min((ks[-1] + 1) * FINE, lags)
        copy = pltpu.make_async_copy(
            buf.at[:, lag0:lag1], out_ref.at[:, lag0:lag1], sems.at[n]
        )
        copy.start()
        copies.append(copy)
    for copy in copies:
        copy.wait()


def correlate(parts, near, far, lengths, steps, flip, carry=None):
    _, rows, chans = parts[0].shape
    _, nsrc, half = near.shape
    samp = 2 * half
    n_parts = len(parts)
    lags, blocks, _, _, tail, rows = plan(samp)
    groups = -(-blocks // GROUP)
    ends = -(-n_parts * tail // LANES) * LANES
    first = carry is None
    work = [
        pltpu.VMEM((nsrc * FINE, n_parts * samp + ends), jnp.bfloat16),
        pltpu.VMEM((nsrc * FINE, LANES), jnp.float32),
    ]
    if first:
        shape = (groups, nsrc * FINE, GROUP * chans)
    else:
        shape = (steps, lags, nsrc // steps, chans)
        work = [pltpu.VMEM(shape, jnp.float32)] + work + [pltpu.SemaphoreType.DMA((groups,))]
    return pl.pallas_call(
        functools.partial(correlate_kernel, n_parts, flip, first, steps),
        out_shape=jax.ShapeDtypeStruct(shape, jnp.float32),
        in_specs=[SMEM] + [VMEM] * (2 + n_parts) + ([] if first else [VMEM]),
        out_specs=VMEM if first else HBM,
        scratch_shapes=work,
        compiler_params=LARGE,
        cost_estimate=pl.CostEstimate(
            flops=2 * nsrc * FINE * blocks * chans * samp * n_parts, bytes_accessed=8 << 20, transcendentals=0
        ),
        name="correlate",
    )(lengths, near, far, *parts, *([] if first else [carry]))


def swap(value, axis, size, distance):
    return lax.ppermute(value, axis, [(i, i ^ distance) for i in range(size)])


def shards(n_tm, n_far, traces, lengths, source_blocks):
    steps = source_blocks.shape[0]
    sent, owners = extract(traces, source_blocks, n_tm)
    got = lax.all_to_all(sent, ("tm", "zl", "x"), 0, 0)
    held = pick(got, owners, n_tm)
    bit = 1
    while bit < n_far:
        came = swap(held, "zh", n_far, bit)
        held = choose(held, came, owners, bit)
        bit *= 2
    near = held
    far = swap(near, "zl", 2, 1)
    near_x = swap(near, "x", 2, 1)
    far_x = swap(far, "x", 2, 1)
    blocks = {0: traces}
    bit = n_tm // 2
    while bit:
        for m in list(blocks):
            blocks[m | bit] = swap(blocks[m], "tm", n_tm, bit)
        bit //= 2
    parts = []
    for m in range(n_tm):
        parts.append(prepare(blocks[m], lengths, m))
    carry = correlate(parts, near, far, lengths, steps, 0)
    out = correlate(parts, near_x, far_x, lengths, steps, 1, carry)
    return jnp.transpose(out, (2, 0, 1, 3))


def solution(mesh):
    n_tm, n_chan = mesh.shape["tm"], mesh.shape["chan"]
    split = Mesh(
        mesh.devices.reshape(n_tm, n_chan // NEAR, 2, 2), ("tm", "zh", "zl", "x")
    )
    chan = ("zh", "zl", "x")
    return jax.shard_map(
        functools.partial(shards, n_tm, n_chan // NEAR),
        mesh=split,
        in_specs=(P("tm", chan, None), P(), P()),
        out_specs=P("tm", None, None, chan),
        check_vma=False,
    )
```

time: 1530 us -> 52 us (0.03)
  local copies, waits for them, and re-layouts: 1260 us -> 2.4 us
  waiting for transfers between devices: 96.7 us -> 14.6 us
  matrix products: 64.7 us -> 0 us
  blocking collectives: 47.3 us -> 0 us
  other arithmetic: 28.5 us -> 0 us
  between operations: 22.4 us -> 0.1 us
  Pallas kernels: 0 us -> 21.5 us
    gather x1809 -> x0, local copies, waits for them, and re-layouts: 1210 us -> none
    unnamed x2 -> x0, waiting for transfers between devices: 96.7 us -> none
    dot_general x9 -> x0, matrix products: 64.7 us -> none  [correlate(): jnp.einsum('gnau,gcu->gnac', shifted, receivers, preferred_element_type=j...]
    psum x1 -> x0, blocking collectives: 47.3 us -> none  [shards(): summed = lax.psum(jnp.stack(contributions), 'chan')]
    unnamed x16 -> x6, local copies, waits for them, and re-layouts: 41.1 us -> 2.4 us
    reduce_sum x2 -> x0, other arithmetic: 23.3 us -> none  [the longest x1 22 us: correlate(): jnp.sum(product / root_count[:, None, None, None], axis=0)]
    pallas_call x0 -> x9, Pallas kernels: none -> 21.5 us  [the longest x2 15.2 us: correlate(): pl.pallas_call(functools.partial(correlate_kernel, n_parts, flip, first,...]
  transfers between devices with their start and end apart: 1 -> 8, of which waited for: 1 -> 3; matrix products, arithmetic and copies ran while one was open for 0% -> 0% of each run, Pallas kernels for 0% -> 26%
where the time goes in v1:
time: 52 us; the launch traced here: 51.6 us
  Pallas kernels  21.5 us (41%)
  waiting for transfers between devices  14.6 us (28%)
  starting transfers between devices  13.1 us (25%)
  local copies, waits for them, and re-layouts  2.4 us (5%)
    pallas_call x2, Pallas kernels, correlate(): pl.pallas_call(functools.partial(correlate_kernel, n_parts, flip, first,...  15.2 us
    ppermute x7, waiting for transfers between devices, swap(): return lax.ppermute(value, axis, [(i, i ^ distance) for i in range(size)])  14.3 us
    ppermute x7, starting transfers between devices, swap(): return lax.ppermute(value, axis, [(i, i ^ distance) for i in range(size)])  9.17 us
    all_to_all x1, starting transfers between devices, shards(): got = lax.all_to_all(sent, ('tm', 'zl', 'x'), 0, 0)  3.9 us
    pallas_call x4, Pallas kernels, prepare(): pl.pallas_call(functools.partial(prepare_kernel, distance), out_shape=jax...  3.66 us
    pallas_call x1, Pallas kernels, extract(): pl.pallas_call(functools.partial(extract_kernel, chans // SRC), out_shape...  2.48 us
    unnamed x6, local copies, waits for them, and re-layouts  2.4 us
  transfers between devices with their start and end apart: 8, of which 3 were waited for; matrix products, arithmetic and copies ran while one was open for 0% of the time, Pallas kernels for 26%

profile of v1, /device:TPU:0, one launch (start us, length us, event | category | flops | bytes accessed | tf_op | source)
XLA Modules:
  0.0 51.6 jit_solution(3506654050286028062)
XLA Ops:
  0.0 3.0 %collective-permute-start.5 = (bf16[2,128,1024]{2,1,0:T(8,128)(2,1)}, bf16[2,128,1024]{2,1,0:T(8,128)(2,1)S(1)}, u32[]{:S(2)}, u32[]{:S(2)}) collective-permute-start(bf16[2,128,1024]{2,1,0:T(8,128)(2,1)} %part_ref.1), channel_id=1, source_target_pairs={{0,16},{8,24},{16,0},{24,8},{1,17},{9,25},{17,1},{25,9},{2,18},{10... | collective-permute-start | bytes 1572872 | tf_op jit(solution)/shard_map/ppermute | solution.py:289
  3.0 2.5 %extract.1 = (bf16[16,24,512]{2,1,0:T(8,128)(2,1)}, s32[3,8,128]{2,1,0:T(8,128)}) custom-call(s32[3]{0:T(128)} %blocks_hbm.1, bf16[2,128,1024]{2,1,0:T(8,128)(2,1)} %part_ref.1), custom_call_target="tpu_custom_call" | custom-call | tf_op jit(solution)/shard_map/extract/pallas_call | solution.py:71
  5.5 3.9 %all-to-all-start = ((bf16[16,24,512]{2,1,0:T(8,128)(2,1)}), bf16[16,24,512]{2,1,0:T(8,128)(2,1)S(1)}, u32[]{:S(2)}, u32[]{:S(2)}) async-start(bf16[16,24,512]{2,1,0:T(8,128)(2,1)} %get-tuple-element.8), calls=%async_computation | async-start | bytes 786432 | tf_op jit(solution)/shard_map/all_to_all | solution.py:295
  9.4 0.4 collective-permute-start.4
  9.8 9.0 %collective-permute-done.5.part_ref = bf16[2,128,1024]{2,1,0:T(8,128)(2,1)S(1)} collective-permute-done((bf16[2,128,1024]{2,1,0:T(8,128)(2,1)}, bf16[2,128,1024]{2,1,0:T(8,128)(2,1)S(1)}, u32[]{:S(2)}, u32[]{:S(2)}) %collective-permute-start.5) | collective-permute-done | bytes 524320 | tf_op jit(solution)/shard_map/ppermute | solution.py:289
  18.8 0.0 collective-permute-start.6
  18.8 0.3 all-to-all-done.got_ref
  19.1 0.0 copy-start.1
  19.1 0.7 %copy-done.1 = s32[3,8,128]{2,1,0:T(8,128)S(1)} copy-done((s32[3,8,128]{2,1,0:T(8,128)S(1)}, s32[3,8,128]{2,1,0:T(8,128)}, u32[]{:S(2)}) %copy-start.1) | copy-done | bytes 12312
  19.8 0.1 pick.1.held_ref
  19.8 2.9 %collective-permute-start = (bf16[4,24,512]{2,1,0:T(8,128)(2,1)S(1)}, bf16[4,24,512]{2,1,0:T(8,128)(2,1)S(1)}, u32[]{:S(2)}, u32[]{:S(2)}) collective-permute-start(bf16[4,24,512]{2,1,0:T(8,128)(2,1)S(1)} %pick.1.held_ref), channel_id=1, source_target_pairs={{0,4},{4,0},{1,5},{5,1},{2,6},{6,2},{3,7},{7,3},{8,12},{12,8},{9,1... | collective-permute-start | bytes 294920 | tf_op jit(solution)/shard_map/ppermute | solution.py:289
  22.7 5.3 %collective-permute-done.came_ref = bf16[4,24,512]{2,1,0:T(8,128)(2,1)S(1)} collective-permute-done((bf16[4,24,512]{2,1,0:T(8,128)(2,1)S(1)}, bf16[4,24,512]{2,1,0:T(8,128)(2,1)S(1)}, u32[]{:S(2)}, u32[]{:S(2)}) %collective-permute-start) | collective-permute-done | bytes 98336 | tf_op jit(solution)/shard_map/ppermute | solution.py:289
  28.1 0.8 %collective-permute-start.2 = (bf16[4,24,512]{2,1,0:T(8,128)(2,1)S(1)}, bf16[4,24,512]{2,1,0:T(8,128)(2,1)S(1)}, u32[]{:S(2)}, u32[]{:S(2)}) collective-permute-start(bf16[4,24,512]{2,1,0:T(8,128)(2,1)S(1)} %choose.1.near_ref), channel_id=1, source_target_pairs={{0,2},{2,0},{1,3},{3,1},{4,6},{6,4},{5,7},{7,5},{8,10},{10,8},{9,1... | collective-permute-start | bytes 294920 | tf_op jit(solution)/shard_map/ppermute | solution.py:289
  28.9 0.0 copy-start
  28.9 1.0 %copy-done = bf16[2,128,1024]{2,1,0:T(8,128)(2,1)S(1)} copy-done((bf16[2,128,1024]{2,1,0:T(8,128)(2,1)S(1)}, bf16[2,128,1024]{2,1,0:T(8,128)(2,1)}, u32[]{:S(2)}) %copy-start) | copy-done | bytes 524312
  29.9 0.0 copy-start.2
  29.9 0.7 %copy-done.2 = s32[8]{0:T(128)S(1)} copy-done((s32[8]{0:T(128)S(1)}, s32[8]{0:T(128)}, u32[]{:S(2)}) %copy-start.2) | copy-done | bytes 56
  30.6 0.9 %prepare.4.refs_0_ = bf16[2,1248,128]{2,1,0:T(8,128)(2,1)S(1)} custom-call(s32[8]{0:T(128)S(1)} %copy-done.2, bf16[2,128,1024]{2,1,0:T(8,128)(2,1)S(1)} %copy-done), custom_call_target="tpu_custom_call" | custom-call | bytes 4194304 | tf_op jit(solution)/shard_map/prepare/pallas_call | solution.py:159
  31.5 0.9 %prepare.6.refs_2_ = bf16[2,1248,128]{2,1,0:T(8,128)(2,1)S(1)} custom-call(s32[8]{0:T(128)S(1)} %copy-done.2, bf16[2,128,1024]{2,1,0:T(8,128)(2,1)S(1)} %collective-permute-done.5.part_ref), custom_call_target="tpu_custom_call" | custom-call | bytes 4194304 | tf_op jit(solution)/shard_map/prepare/pallas_call | solution.py:159
  32.4 0.0 collective-permute-done.4.part_ref
  32.4 0.9 %prepare.5.refs_1_ = bf16[2,1248,128]{2,1,0:T(8,128)(2,1)S(1)} custom-call(s32[8]{0:T(128)S(1)} %copy-done.2, bf16[2,128,1024]{2,1,0:T(8,128)(2,1)S(1)} %collective-permute-done.4.part_ref), custom_call_target="tpu_custom_call" | custom-call | bytes 4194304 | tf_op jit(solution)/shard_map/prepare/pallas_call | solution.py:159
  33.3 1.6 %collective-permute-start.1 = (bf16[4,24,512]{2,1,0:T(8,128)(2,1)S(1)}, bf16[4,24,512]{2,1,0:T(8,128)(2,1)S(1)}, u32[]{:S(2)}, u32[]{:S(2)}) collective-permute-start(bf16[4,24,512]{2,1,0:T(8,128)(2,1)S(1)} %choose.1.near_ref), channel_id=1, source_target_pairs={{0,1},{1,0},{2,3},{3,2},{4,5},{5,4},{6,7},{7,6},{8,9},{9,8},{10,11... | collective-permute-start | bytes 294920 | tf_op jit(solution)/shard_map/ppermute | solution.py:289
  34.9 0.0 collective-permute-done.2.far_ref
  34.9 0.5 %collective-permute-start.3 = (bf16[4,24,512]{2,1,0:T(8,128)(2,1)S(1)}, bf16[4,24,512]{2,1,0:T(8,128)(2,1)S(1)}, u32[]{:S(2)}, u32[]{:S(2)}) collective-permute-start(bf16[4,24,512]{2,1,0:T(8,128)(2,1)S(1)} %collective-permute-done.2.far_ref), channel_id=1, source_target_pairs={{0,1},{1,0},{2,3},{3,2},{4,5},{5,4},{6,7},{7,6},{8,9},{9,8},{10,11... | collective-permute-start | bytes 294920 | tf_op jit(solution)/shard_map/ppermute | solution.py:289
  35.4 0.0 collective-permute-done.6.part_ref
  35.4 0.9 %prepare.7.refs_3_ = bf16[2,1248,128]{2,1,0:T(8,128)(2,1)S(1)} custom-call(s32[8]{0:T(128)S(1)} %copy-done.2, bf16[2,128,1024]{2,1,0:T(8,128)(2,1)S(1)} %collective-permute-done.6.part_ref), custom_call_target="tpu_custom_call" | custom-call | bytes 4194304 | tf_op jit(solution)/shard_map/prepare/pallas_call | solution.py:159
  36.4 7.3 %correlate.2.refs_4_ = f32[7,384,256]{2,1,0:T(8,128)S(1)} custom-call(s32[8]{0:T(128)S(1)} %copy-done.2, bf16[4,24,512]{2,1,0:T(8,128)(2,1)S(1)} %choose.1.near_ref, bf16[4,24,512]{2,1,0:T(8,128)(2,1)S(1)} %collective-permute-done.2.far_ref, bf16[2,1248,128]{2,1,0:T(8,128)(2,1)S(1)} %prepare.4.refs_0_, bf16[2,1248,128]{2,1,0:T(8,128)(2,1)S(1)} %prepare.5.refs_1_, ...), custom_call_target="tpu_custom_call" | custom-call | flops 5234491392 | bytes 8388608 | tf_op jit(solution)/shard_map/correlate/pallas_call | solution.py:274
  43.7 0.0 collective-permute-done.1.near_ref
  43.7 0.0 collective-permute-done.3.far_ref
  43.7 8.0 %correlate.3 = f32[3,201,8,128]{3,2,1,0:T(8,128)} custom-call(s32[8]{0:T(128)S(1)} %copy-done.2, bf16[4,24,512]{2,1,0:T(8,128)(2,1)S(1)} %collective-permute-done.1.near_ref, bf16[4,24,512]{2,1,0:T(8,128)(2,1)S(1)} %collective-permute-done.3.far_ref, bf16[2,1248,128]{2,1,0:T(8,128)(2,1)S(1)} %prepare.4.refs_0_, bf16[2,1248,128]{2,1,0:T(8,128)(2,1)S(1)} %prepare.5.refs_1_, ...), custom_call_target="tpu_custom_call" | custom-call | flops 5234491392 | bytes 8388608 | tf_op jit(solution)/shard_map/correlate/pallas_call | solution.py:274
  (1 shorter events, 0.0 us)
Async XLA Ops:
  0.0 18.8 %collective-permute-start.5 = (bf16[2,128,1024]{2,1,0:T(8,128)(2,1)}, bf16[2,128,1024]{2,1,0:T(8,128)(2,1)S(1)}, u32[]{:S(2)}, u32[]{:S(2)}) collective-permute-start(bf16[2,128,1024]{2,1,0:T(8,128)(2,1)} %part_ref.1), channel_id=1, source_target_pairs={{0,16},{8,24},{16,0},{24,8},{1,17},{9,25},{17,1},{25,9},{2,18},{10... | collective-permute-start | bytes 1572872 | tf_op jit(solution)/shard_map/ppermute | solution.py:289
  5.5 13.6 %all-to-all-start = ((bf16[16,24,512]{2,1,0:T(8,128)(2,1)}), bf16[16,24,512]{2,1,0:T(8,128)(2,1)S(1)}, u32[]{:S(2)}, u32[]{:S(2)}) async-start(bf16[16,24,512]{2,1,0:T(8,128)(2,1)} %get-tuple-element.8), calls=%async_computation | async-start | bytes 786432 | tf_op jit(solution)/shard_map/all_to_all | solution.py:295
  9.4 23.0 %collective-permute-start.4 = (bf16[2,128,1024]{2,1,0:T(8,128)(2,1)}, bf16[2,128,1024]{2,1,0:T(8,128)(2,1)S(1)}, u32[]{:S(2)}, u32[]{:S(2)}) collective-permute-start(bf16[2,128,1024]{2,1,0:T(8,128)(2,1)} %part_ref.1), channel_id=1, source_target_pairs={{0,8},{8,0},{16,24},{24,16},{1,9},{9,1},{17,25},{25,17},{2,10},{10... | collective-permute-start | bytes 1572872 | tf_op jit(solution)/shard_map/ppermute | solution.py:289
  18.8 16.6 %collective-permute-start.6 = (bf16[2,128,1024]{2,1,0:T(8,128)(2,1)S(1)}, bf16[2,128,1024]{2,1,0:T(8,128)(2,1)S(1)}, u32[]{:S(2)}, u32[]{:S(2)}) collective-permute-start(bf16[2,128,1024]{2,1,0:T(8,128)(2,1)S(1)} %collective-permute-done.5.part_ref), channel_id=1, source_target_pairs={{0,8},{8,0},{16,24},{24,16},{1,9},{9,1},{17,25},{25,17},{2,10},{10... | collective-permute-start | bytes 1572872 | tf_op jit(solution)/shard_map/ppermute | solution.py:289
  19.1 0.7 %copy-start.1 = (s32[3,8,128]{2,1,0:T(8,128)S(1)}, s32[3,8,128]{2,1,0:T(8,128)}, u32[]{:S(2)}) copy-start(s32[3,8,128]{2,1,0:T(8,128)} %get-tuple-element.7.owner_ref) | copy-start | bytes 36868
  19.8 8.2 %collective-permute-start = (bf16[4,24,512]{2,1,0:T(8,128)(2,1)S(1)}, bf16[4,24,512]{2,1,0:T(8,128)(2,1)S(1)}, u32[]{:S(2)}, u32[]{:S(2)}) collective-permute-start(bf16[4,24,512]{2,1,0:T(8,128)(2,1)S(1)} %pick.1.held_ref), channel_id=1, source_target_pairs={{0,4},{4,0},{1,5},{5,1},{2,6},{6,2},{3,7},{7,3},{8,12},{12,8},{9,1... | collective-permute-start | bytes 294920 | tf_op jit(solution)/shard_map/ppermute | solution.py:289
  28.1 6.8 %collective-permute-start.2 = (bf16[4,24,512]{2,1,0:T(8,128)(2,1)S(1)}, bf16[4,24,512]{2,1,0:T(8,128)(2,1)S(1)}, u32[]{:S(2)}, u32[]{:S(2)}) collective-permute-start(bf16[4,24,512]{2,1,0:T(8,128)(2,1)S(1)} %choose.1.near_ref), channel_id=1, source_target_pairs={{0,2},{2,0},{1,3},{3,1},{4,6},{6,4},{5,7},{7,5},{8,10},{10,8},{9,1... | collective-permute-start | bytes 294920 | tf_op jit(solution)/shard_map/ppermute | solution.py:289
  28.9 1.0 %copy-start = (bf16[2,128,1024]{2,1,0:T(8,128)(2,1)S(1)}, bf16[2,128,1024]{2,1,0:T(8,128)(2,1)}, u32[]{:S(2)}) copy-start(bf16[2,128,1024]{2,1,0:T(8,128)(2,1)} %part_ref.1) | copy-start | bytes 1572868
  29.9 0.7 %copy-start.2 = (s32[8]{0:T(128)S(1)}, s32[8]{0:T(128)}, u32[]{:S(2)}) copy-start(s32[8]{0:T(128)} %len_ref.11) | copy-start | bytes 100
  33.3 10.3 %collective-permute-start.1 = (bf16[4,24,512]{2,1,0:T(8,128)(2,1)S(1)}, bf16[4,24,512]{2,1,0:T(8,128)(2,1)S(1)}, u32[]{:S(2)}, u32[]{:S(2)}) collective-permute-start(bf16[4,24,512]{2,1,0:T(8,128)(2,1)S(1)} %choose.1.near_ref), channel_id=1, source_target_pairs={{0,1},{1,0},{2,3},{3,2},{4,5},{5,4},{6,7},{7,6},{8,9},{9,8},{10,11... | collective-permute-start | bytes 294920 | tf_op jit(solution)/shard_map/ppermute | solution.py:289
  34.9 8.8 %collective-permute-start.3 = (bf16[4,24,512]{2,1,0:T(8,128)(2,1)S(1)}, bf16[4,24,512]{2,1,0:T(8,128)(2,1)S(1)}, u32[]{:S(2)}, u32[]{:S(2)}) collective-permute-start(bf16[4,24,512]{2,1,0:T(8,128)(2,1)S(1)} %collective-permute-done.2.far_ref), channel_id=1, source_target_pairs={{0,1},{1,0},{2,3},{3,2},{4,5},{5,4},{6,7},{7,6},{8,9},{9,8},{10,11... | collective-permute-start | bytes 294920 | tf_op jit(solution)/shard_map/ppermute | solution.py:289
